TPU v7x, 32 devices: a whole 2x2x4 slice. The times are simulated.
32 devices in a mesh: wave: 8 (over z, y), lev: 4 (over x, core).
Axes of the slice: x: 2, y: 2, z: 4, core: 2. Of those that a mesh axis runs over, the one named last changes fastest.
Arguments:
- fine_state: float32 [8, 3, 2, 24, 49], P('lev', None, None, 'wave'), may hold values from -6 to 6
- fold_pairs: int32 [24], replicated, may hold values from 0 to 23, each once
- legendre: bfloat16 [24, 96, 49], P('wave', 'lev'), may hold values from -0.875 to 0.875
- gauss_weights: float32 [96], P('lev'), may hold values from 0.5 to 3
- grid_coef: float32 [8, 2560], replicated, may hold values from -4 to 4
- modes_from: float32 [8, 8], replicated
- modes_to: float32 [8, 8], replicated, as said below
- mode_rates: float32 [8], replicated, may hold values from 0.2 to 20
Outputs:
- corrected: float32 [8, 2, 2, 24, 49], P('lev', None, None, 'wave')
- fine_tend: float32 [8, 3, 2, 24, 49], P('lev', None, None, 'wave')
Inputs may be any that keep to these rules, and one draw needn't show every extreme that they name: Slot p holds zonal wavenumbers fold_pairs[p] and 47 - fold_pairs[p]; every value occurs once. modes_to is the inverse of modes_from.
All inputs are finite; a program needn't handle non-finite values.
Results may differ from a plain program's by a relative error of at most 0.02.
Values may be sent and summed in bfloat16 or wider, within the bound.
No kernel may reach another device: no remote copies, remote signals or barrier semaphores. Data moves between devices by JAX's collectives and lax.ppermute only.
A program may use at most 64 MiB of HBM per device.

v0:
```python
import math
import jax
import jax.numpy as jnp
from jax import lax
from jax.sharding import PartitionSpec as P

STEP_HALF = 0.5
quad_weights = ((5.0 / 24.0, 1.0 / 3.0, -1.0 / 24.0), (-1.0 / 24.0, 1.0 / 3.0, 5.0 / 24.0))
HIGHEST = lax.Precision.HIGHEST


def fourier_table(waves, points, amplitude):
    steps = jnp.arange(points, dtype=jnp.int32)
    turns = waves[:, :, None] * steps[None, None, :] % points
    angles = turns.astype(jnp.float32) * (2.0 * math.pi / points)
    return jnp.stack([jnp.cos(angles) * amplitude, -jnp.sin(angles) * amplitude]).astype(
        jnp.bfloat16
    )


def fine_rows(small_wave, fine_width):
    row_ids = jnp.arange(fine_width + 1, dtype=jnp.int32)[None, :]
    return row_ids < fine_width - small_wave[:, None]


def coarse_rows(small_wave, coarse):
    row_ids = jnp.arange(coarse, dtype=jnp.int32)[None, :]
    coarse_keep = row_ids < coarse - small_wave[:, None]
    degree = (small_wave[:, None] + row_ids).astype(jnp.float32)
    return (coarse_keep, degree)


def legendre_inverse(spectral, legendre_table, row_mask):
    split_spec = spectral[:, :, :, :, None, :] * row_mask[None, None, None]
    return jnp.einsum(
        "abcpmr,plr->abcpml", split_spec, legendre_table, preferred_element_type=jnp.float32
    ).astype(jnp.bfloat16)


def legendre_forward(returned, legendre_table, row_mask):
    members = jnp.einsum(
        "abcpml,plr->abcpmr", returned, legendre_table, preferred_element_type=jnp.float32
    )
    return jnp.sum(members * row_mask.astype(jnp.float32)[None, None, None], axis=4)


def grid_step(fourier, wave_table, coef, weights, factor):
    grid_field = jnp.einsum(
        "abcpmz,cpmk->abzk", fourier, wave_table, preferred_element_type=jnp.float32
    )
    product = (coef[:, None, None, :] * grid_field * grid_field).astype(jnp.bfloat16)
    returned = jnp.einsum(
        "abzk,cpmk->abcpmz", product, wave_table, preferred_element_type=jnp.float32
    )
    return (returned * (weights * factor)).astype(jnp.bfloat16)


def mix(matrix, values):
    return jnp.einsum("ql,lbcpr->qbcpr", matrix, values, precision=HIGHEST)


def per_device(
    fine_state, fold_pairs, legendre, gauss_weights, grid_coef, modes_from, modes_to, mode_rates
):
    n_wave = lax.axis_size("wave")
    wave_idx = lax.axis_index("wave")
    lev_idx = lax.axis_index("lev")
    lev_dev = fine_state.shape[0]
    pairs_dev = fine_state.shape[3]
    fine_width = fine_state.shape[4] - 1
    coarse = fine_width // 2
    longitudes = grid_coef.shape[1]
    band_size = legendre.shape[1] // n_wave
    small_wave = lax.dynamic_slice_in_dim(fold_pairs, wave_idx * pairs_dev, pairs_dev)
    first_member = fine_rows(small_wave, fine_width)
    member_mask = jnp.stack([first_member, jnp.logical_not(first_member)], 1).astype(jnp.bfloat16)
    coarse_keep, degree = coarse_rows(small_wave, coarse)
    keep_mask = coarse_keep[:, None, :].astype(jnp.bfloat16)
    keep_float = coarse_keep.astype(jnp.float32)
    fine_table = fourier_table(
        jnp.stack([fold_pairs, fine_width - 1 - fold_pairs], 1), longitudes, fine_width ** (-0.5)
    )
    coarse_table = fourier_table(fold_pairs[:, None], longitudes // 2, coarse ** (-0.5))
    coarse_leg = legendre[:, :, :coarse]
    coarse_coef = grid_coef[:, ::2]
    band_gauss = lax.dynamic_slice_in_dim(gauss_weights, wave_idx * band_size, band_size)
    local_to = lax.dynamic_slice_in_dim(modes_to, lev_idx * lev_dev, lev_dev, 1)
    local_from = lax.dynamic_slice_in_dim(modes_from, lev_idx * lev_dev, lev_dev, 1)
    mode_decay = lax.dynamic_slice_in_dim(mode_rates, lev_idx * lev_dev, lev_dev)

    def project(partial_sum):
        return mix(modes_to, partial_sum)

    def coarse_start(modes):
        gathered = lax.all_gather(modes, "lev", axis=0, tiled=True)
        levels = (mix(modes_from, gathered) * keep_float).astype(jnp.bfloat16)
        return legendre_inverse(levels, coarse_leg, keep_mask)

    def coarse_grid_step(fourier):
        return grid_step(
            fourier, coarse_table, coarse_coef, band_gauss, 2.0 * coarse / (longitudes // 2)
        )

    def coarse_finish(returned):
        partial_sum = legendre_forward(returned, coarse_leg, keep_mask)
        return lax.psum_scatter(
            project(partial_sum).astype(jnp.bfloat16), "lev", scatter_dimension=0, tiled=True
        ).astype(jnp.float32)

    def coarse_eval(modes):
        fourier = lax.all_to_all(
            coarse_start(modes), "wave", split_axis=5, concat_axis=3, tiled=True
        )
        returned = lax.all_to_all(
            coarse_grid_step(fourier), "wave", split_axis=3, concat_axis=5, tiled=True
        )
        return coarse_finish(returned)

    restricted = fine_state[..., :coarse] * keep_float
    fine_spec = lax.all_gather(fine_state.astype(jnp.bfloat16), "lev", axis=0, tiled=True)
    fine_fourier = legendre_inverse(fine_spec, legendre, member_mask)
    fine_fourier = lax.all_to_all(fine_fourier, "wave", split_axis=5, concat_axis=3, tiled=True)
    fine_back = lax.all_to_all(
        grid_step(fine_fourier, fine_table, grid_coef, band_gauss, 2.0 * fine_width / longitudes),
        "wave",
        split_axis=3,
        concat_axis=5,
        tiled=True,
    )
    fine_tend = lax.psum_scatter(
        legendre_forward(fine_back, legendre, member_mask).astype(jnp.bfloat16),
        "lev",
        scatter_dimension=0,
        tiled=True,
    ).astype(jnp.float32)
    restricted_tend = fine_tend[..., :coarse] * keep_float
    stacked = jnp.concatenate([restricted, restricted_tend], 1)
    both_modes = lax.psum_scatter(
        mix(local_to, stacked).astype(jnp.bfloat16), "lev", scatter_dimension=0, tiled=True
    ).astype(jnp.float32)
    nodes = fine_state.shape[1]
    old_state = both_modes[:, :nodes]
    old_tend = both_modes[:, nodes:]
    old_coarse = coarse_eval(old_state[:, 1:2])
    stiffness = (
        mode_decay[:, None, None, None]
        * (degree * (degree + 1.0) / (coarse * (coarse + 1.0)))[None, None]
    )
    source = old_tend - stiffness[:, None] * old_state
    integral_mid = (
        quad_weights[0][0] * source[:, 0]
        + quad_weights[0][1] * source[:, 1]
        + quad_weights[0][2] * source[:, 2]
    )
    integral_end = (
        quad_weights[1][0] * source[:, 0]
        + quad_weights[1][1] * source[:, 1]
        + quad_weights[1][2] * source[:, 2]
    )
    divisor = 1.0 + STEP_HALF * stiffness
    next_mid = (old_state[:, 0] + STEP_HALF * stiffness * old_state[:, 1] + integral_mid) / divisor
    coarse_fresh = coarse_eval(next_mid[:, None])
    next_end = (
        next_mid
        + STEP_HALF * (coarse_fresh[:, 0] - old_coarse[:, 0])
        + STEP_HALF * stiffness * old_state[:, 2]
        + integral_end
    ) / divisor
    change = jnp.stack([next_mid - old_state[:, 1], next_end - old_state[:, 2]], 1)
    lifted = lax.psum_scatter(
        mix(local_from, change).astype(jnp.bfloat16), "lev", scatter_dimension=0, tiled=True
    ).astype(jnp.float32)
    corrected = fine_state[:, 1:] + jnp.pad(
        lifted, ((0, 0), (0, 0), (0, 0), (0, 0), (0, fine_width + 1 - coarse))
    )
    return (corrected, fine_tend)


def solution(mesh):
    placed = (
        P("lev", None, None, "wave", None),
        P(),
        P("wave", "lev", None),
        P("lev"),
        P(),
        P(),
        P(),
        P(),
    )
    return jax.shard_map(
        per_device,
        mesh=mesh,
        in_specs=placed,
        out_specs=(P("lev", None, None, "wave", None), P("lev", None, None, "wave", None)),
        check_vma=False,
    )
```

profile of v0, /device:TPU:0, one launch (start us, length us, event | category | flops | bytes accessed | tf_op | source)
XLA Modules:
  0.0 130.4 jit_solution(1549815140402897033)
XLA Ops:
  0.6 0.0 copy-start
  0.7 0.7 broadcast_subtract_fusion.1
  1.4 0.1 iota_compare_fusion.1
  1.5 6.2 %all_gather.9 = bf16[8,3,2,3,49]{4,2,3,1,0:T(2,128)(2,1)S(1)} all-gather(bf16[2,3,2,3,49]{4,2,3,1,0:T(2,128)(2,1)S(1)} %convert_element_type.212), channel_id=1, replica_groups=mesh['wave'=8,'lev'=4] {'lev'}, dimensions={0}, use_global_device_ids=true | all-gather | bytes 17640 | tf_op jit(solution)/shard_map/all_gather | solution.py:120
  7.7 0.7 copy-done.1
  8.4 0.1 fusion.2
  8.6 0.2 copy.95
  8.7 0.8 reshape.468
  9.6 6.4 %all-to-all-start = ((bf16[8,2,432]{2,1,0:T(2,128)(2,1)}), bf16[8,2,432]{2,1,0:T(2,128)(2,1)S(1)}, u32[]{:S(2)}, u32[]{:S(2)}) async-start(bf16[8,2,432]{2,1,0:T(2,128)(2,1)} %reshape.468), calls=%async_computation | async-start | bytes 32768 | tf_op jit(solution)/shard_map/all_to_all | solution.py:122
  16.0 0.1 fusion.97
  16.1 0.6 multiply_convert_fusion.3
  16.7 2.3 %multiply_convert_fusion.1 = (bf16[1,24,2,2560]{3,1,2,0:T(8,128)(2,1)S(1)}, bf16[1,24,2,2560]{3,1,2,0:T(8,128)(2,1)S(1)}) fusion(s32[24,2]{0,1:T(2,128)S(1)} %pad_add_fusion), kind=kLoop, calls=%fused_computation.52 | loop fusion | flops 1720320 | bytes 491712 | tf_op jit(solution)/shard_map/convert.4
  19.1 0.6 copy-done.6
  19.7 0.1 dynamic_slice.19
  19.8 0.1 broadcast_multiply_fusion
  19.9 0.6 copy-done.7
  20.4 0.1 dynamic-slice_multiply_fusion
  20.5 2.1 %all-to-all-done = bf16[8,2,432]{2,1,0:T(2,128)(2,1)S(1)} async-done(((bf16[8,2,432]{2,1,0:T(2,128)(2,1)}), bf16[8,2,432]{2,1,0:T(2,128)(2,1)S(1)}, u32[]{:S(2)}, u32[]{:S(2)}) %all-to-all-start) | async-done | bytes 13856 | tf_op jit(solution)/shard_map/all_to_all | solution.py:122
  22.6 0.2 reshape.469
  22.8 0.2 copy.97
  23.0 0.7 copy-done.3
  23.7 0.8 fusion.3
  24.6 0.2 copy.99
  24.7 0.8 reshape.470
  25.6 3.9 %all-to-all-start.1 = ((bf16[8,2,432]{2,1,0:T(2,128)(2,1)}), bf16[8,2,432]{2,1,0:T(2,128)(2,1)S(1)}, u32[]{:S(2)}, u32[]{:S(2)}) async-start(bf16[8,2,432]{2,1,0:T(2,128)(2,1)} %reshape.470), calls=%async_computation.1 | async-start | bytes 32768 | tf_op jit(solution)/shard_map/all_to_all | solution.py:123
  29.5 0.1 fusion.110
  29.5 1.4 %slice.58 = f32[8,1280]{1,0:T(8,128)S(1)} slice(f32[8,2560]{1,0:T(8,128)S(1)} %copy-done.3), slice={[0:8:1], [0:2560:2]} | slice | bytes 81920 | tf_op jit(solution)/shard_map/slice | solution.py:85
  31.0 0.6 copy-done.8
  31.6 0.6 dynamic-slice
  32.9 3.2 %all-to-all-done.1 = bf16[8,2,432]{2,1,0:T(2,128)(2,1)S(1)} async-done(((bf16[8,2,432]{2,1,0:T(2,128)(2,1)}), bf16[8,2,432]{2,1,0:T(2,128)(2,1)S(1)}, u32[]{:S(2)}, u32[]{:S(2)}) %all-to-all-start.1) | async-done | bytes 13856 | tf_op jit(solution)/shard_map/all_to_all | solution.py:123
  36.0 0.2 reshape.471
  36.3 0.2 copy.101
  36.4 0.2 fusion
  36.7 10.5 %all-reduce.1 = bf16[8,3,2,3,49]{4,0,3,2,1:T(8,128)(2,1)S(1)} all-reduce(bf16[8,3,2,3,49]{4,0,3,2,1:T(8,128)(2,1)S(1)} %copy.103), channel_id=2, replica_groups=mesh['wave'=8,'lev'=4] {'lev'}, use_global_device_ids=true, to_apply=%region_1.2.clone | all-reduce | flops 7056 | bytes 28224
  47.2 0.3 convolution_convert_fusion
  47.6 11.7 %all-reduce.2 = bf16[8,6,2,3,24]{4,0,3,2,1:T(8,128)(2,1)S(1)} all-reduce(bf16[8,6,2,3,24]{4,0,3,2,1:T(8,128)(2,1)S(1)} %convolution_convert_fusion), channel_id=3, replica_groups=mesh['wave'=8,'lev'=4] {'lev'}, use_global_device_ids=true, to_apply=%region_2.3.clone | all-reduce | flops 6912 | bytes 27648
  59.4 5.2 %all_gather.10 = f32[8,1,2,3,24]{4,2,3,1,0:T(2,128)S(1)} all-gather(f32[2,1,2,3,24]{4,2,3,1,0:T(2,128)S(1)} %copy.104), channel_id=1, replica_groups=mesh['wave'=8,'lev'=4] {'lev'}, dimensions={0}, use_global_device_ids=true | all-gather | bytes 5760 | tf_op jit(solution)/shard_map/all_gather | solution.py:95
  64.6 0.2 fusion.23
  64.8 0.1 fusion.14
  64.9 0.7 copy.106
  65.6 3.3 %all-to-all-start.2 = ((bf16[8,1,2,3,1,24]{0,2,3,4,1,5:T(2,128)(2,1)}), bf16[8,1,2,3,1,24]{0,2,3,4,1,5:T(2,128)(2,1)S(1)}, u32[]{:S(2)}, u32[]{:S(2)}) async-start(bf16[8,1,2,3,1,24]{0,2,3,4,1,5:T(2,128)(2,1)} %copy.106), calls=%async_computation.2 | async-start | bytes 73728 | tf_op jit(solution)/shard_map/all_to_all | solution.py:111
  69.0 5.2 %all_gather.11 = f32[8,1,2,3,24]{4,2,3,1,0:T(2,128)S(1)} all-gather(f32[2,1,2,3,24]{4,2,3,1,0:T(2,128)S(1)} %copy.114), channel_id=1, replica_groups=mesh['wave'=8,'lev'=4] {'lev'}, dimensions={0}, use_global_device_ids=true | all-gather | bytes 5760 | tf_op jit(solution)/shard_map/all_gather | solution.py:95
  74.2 0.2 fusion.20
  74.4 0.1 fusion.16
  74.5 0.6 copy.125
  75.1 0.7 copy.116
  75.8 5.9 %all-to-all-start.4 = ((bf16[8,1,2,3,1,24]{0,2,3,4,1,5:T(2,128)(2,1)}), bf16[8,1,2,3,1,24]{0,2,3,4,1,5:T(2,128)(2,1)S(1)}, u32[]{:S(2)}, u32[]{:S(2)}) async-start(bf16[8,1,2,3,1,24]{0,2,3,4,1,5:T(2,128)(2,1)} %copy.116), calls=%async_computation.4 | async-start | bytes 73728 | tf_op jit(solution)/shard_map/all_to_all | solution.py:111
  81.8 0.4 fusion.21
  82.2 0.8 copy.110
  82.9 5.5 %all-to-all-done.4 = bf16[8,1,2,3,1,24]{0,2,3,4,1,5:T(2,128)(2,1)S(1)} async-done(((bf16[8,1,2,3,1,24]{0,2,3,4,1,5:T(2,128)(2,1)}), bf16[8,1,2,3,1,24]{0,2,3,4,1,5:T(2,128)(2,1)S(1)}, u32[]{:S(2)}, u32[]{:S(2)}) %all-to-all-start.4) | async-done | bytes 2336 | tf_op jit(solution)/shard_map/all_to_all | solution.py:111
  88.4 3.3 %all-to-all-start.3 = ((bf16[8,1,2,24,1,3]{0,2,5,4,1,3:T(2,128)(2,1)}), bf16[8,1,2,24,1,3]{0,2,5,4,1,3:T(2,128)(2,1)S(1)}, u32[]{:S(2)}, u32[]{:S(2)}) async-start(bf16[8,1,2,24,1,3]{0,2,5,4,1,3:T(2,128)(2,1)} %copy.110), calls=%async_computation.3 | async-start | bytes 73728 | tf_op jit(solution)/shard_map/all_to_all | solution.py:114
  91.9 0.4 fusion.18
  92.2 0.7 copy.120
  93.0 5.5 %all-to-all-done.3 = bf16[8,1,2,24,1,3]{0,2,5,4,1,3:T(2,128)(2,1)S(1)} async-done(((bf16[8,1,2,24,1,3]{0,2,5,4,1,3:T(2,128)(2,1)}), bf16[8,1,2,24,1,3]{0,2,5,4,1,3:T(2,128)(2,1)S(1)}, u32[]{:S(2)}, u32[]{:S(2)}) %all-to-all-start.3) | async-done | bytes 2336 | tf_op jit(solution)/shard_map/all_to_all | solution.py:114
  98.4 3.3 %all-to-all-start.5 = ((bf16[8,1,2,24,1,3]{0,2,5,4,1,3:T(2,128)(2,1)}), bf16[8,1,2,24,1,3]{0,2,5,4,1,3:T(2,128)(2,1)S(1)}, u32[]{:S(2)}, u32[]{:S(2)}) async-start(bf16[8,1,2,24,1,3]{0,2,5,4,1,3:T(2,128)(2,1)} %copy.120), calls=%async_computation.5 | async-start | bytes 73728 | tf_op jit(solution)/shard_map/all_to_all | solution.py:114
  101.8 0.2 fusion.7
  102.0 0.2 fusion.15
  102.2 6.2 %all-to-all-done.5 = bf16[8,1,2,24,1,3]{0,2,5,4,1,3:T(2,128)(2,1)S(1)} async-done(((bf16[8,1,2,24,1,3]{0,2,5,4,1,3:T(2,128)(2,1)}), bf16[8,1,2,24,1,3]{0,2,5,4,1,3:T(2,128)(2,1)S(1)}, u32[]{:S(2)}, u32[]{:S(2)}) %all-to-all-start.5) | async-done | bytes 2336 | tf_op jit(solution)/shard_map/all_to_all | solution.py:114
  108.5 0.2 fusion.9
  108.7 0.2 fusion.17
  108.8 10.3 %all-reduce.6 = (bf16[8,1,2,3,24]{4,0,3,2,1:T(8,128)(2,1)S(1)}, bf16[8,1,2,3,24]{4,0,3,2,1:T(8,128)(2,1)S(1)}) all-reduce(bf16[8,1,2,3,24]{4,0,3,2,1:T(8,128)(2,1)S(1)} %fusion.17, bf16[8,1,2,3,24]{4,0,3,2,1:T(8,128)(2,1)S(1)} %fusion.15), channel_id=5, replica_groups=mesh['wave'=8,'lev'=4] {'lev'}, use_global_device_ids=true, to_apply=%region_4.5.clone | all-reduce | flops 2304 | bytes 9216
  119.1 0.2 convolution_convert_fusion.2
  119.4 10.4 %all-reduce.5 = bf16[8,2,2,3,24]{4,0,3,2,1:T(8,128)(2,1)S(1)} all-reduce(bf16[8,2,2,3,24]{4,0,3,2,1:T(8,128)(2,1)S(1)} %convolution_convert_fusion.2), channel_id=6, replica_groups=mesh['wave'=8,'lev'=4] {'lev'}, use_global_device_ids=true, to_apply=%region_5.6.clone | all-reduce | flops 2304 | bytes 9216
  129.8 0.6 copy.124
  (37 shorter events, 0.4 us)
Async XLA Ops:
  0.6 46.6 %copy-start = (f32[8,8]{1,0:T(8,128)S(1)}, f32[8,8]{1,0:T(8,128)}, u32[]{:S(2)}) copy-start(f32[8,8]{1,0:T(8,128)} %param.14) | copy-start | bytes 772
  0.6 0.8 copy-start.2
  7.7 0.7 copy-start.1
  9.6 6.4 %copy-start.5 = (s32[24]{0:T(128)S(1)}, s32[24]{0:T(128)}, u32[]{:S(2)}) copy-start(s32[24]{0:T(128)} %param.9) | copy-start | bytes 292
  9.6 13.0 %all-to-all-start = ((bf16[8,2,432]{2,1,0:T(2,128)(2,1)}), bf16[8,2,432]{2,1,0:T(2,128)(2,1)S(1)}, u32[]{:S(2)}, u32[]{:S(2)}) async-start(bf16[8,2,432]{2,1,0:T(2,128)(2,1)} %reshape.468), calls=%async_computation | async-start | bytes 32768 | tf_op jit(solution)/shard_map/all_to_all | solution.py:122
  19.0 0.7 copy-start.6
  19.8 0.7 copy-start.7
  22.8 0.9 copy-start.3
  25.6 10.5 %all-to-all-start.1 = ((bf16[8,2,432]{2,1,0:T(2,128)(2,1)}), bf16[8,2,432]{2,1,0:T(2,128)(2,1)S(1)}, u32[]{:S(2)}, u32[]{:S(2)}) async-start(bf16[8,2,432]{2,1,0:T(2,128)(2,1)} %reshape.470), calls=%async_computation.1 | async-start | bytes 32768 | tf_op jit(solution)/shard_map/all_to_all | solution.py:123
  31.0 0.7 copy-start.8
  59.3 5.3 %copy-start.4 = (f32[8,8]{1,0:T(8,128)S(1)}, f32[8,8]{1,0:T(8,128)}, u32[]{:S(2)}) copy-start(f32[8,8]{1,0:T(8,128)} %param.13) | copy-start | bytes 772
  65.6 10.2 %all-to-all-start.2 = ((bf16[8,1,2,3,1,24]{0,2,3,4,1,5:T(2,128)(2,1)}), bf16[8,1,2,3,1,24]{0,2,3,4,1,5:T(2,128)(2,1)S(1)}, u32[]{:S(2)}, u32[]{:S(2)}) async-start(bf16[8,1,2,3,1,24]{0,2,3,4,1,5:T(2,128)(2,1)} %copy.106), calls=%async_computation.2 | async-start | bytes 73728 | tf_op jit(solution)/shard_map/all_to_all | solution.py:111
  75.8 12.6 %all-to-all-start.4 = ((bf16[8,1,2,3,1,24]{0,2,3,4,1,5:T(2,128)(2,1)}), bf16[8,1,2,3,1,24]{0,2,3,4,1,5:T(2,128)(2,1)S(1)}, u32[]{:S(2)}, u32[]{:S(2)}) async-start(bf16[8,1,2,3,1,24]{0,2,3,4,1,5:T(2,128)(2,1)} %copy.116), calls=%async_computation.4 | async-start | bytes 73728 | tf_op jit(solution)/shard_map/all_to_all | solution.py:111
  88.4 10.0 %all-to-all-start.3 = ((bf16[8,1,2,24,1,3]{0,2,5,4,1,3:T(2,128)(2,1)}), bf16[8,1,2,24,1,3]{0,2,5,4,1,3:T(2,128)(2,1)S(1)}, u32[]{:S(2)}, u32[]{:S(2)}) async-start(bf16[8,1,2,24,1,3]{0,2,5,4,1,3:T(2,128)(2,1)} %copy.110), calls=%async_computation.3 | async-start | bytes 73728 | tf_op jit(solution)/shard_map/all_to_all | solution.py:114
  98.4 10.0 %all-to-all-start.5 = ((bf16[8,1,2,24,1,3]{0,2,5,4,1,3:T(2,128)(2,1)}), bf16[8,1,2,24,1,3]{0,2,5,4,1,3:T(2,128)(2,1)S(1)}, u32[]{:S(2)}, u32[]{:S(2)}) async-start(bf16[8,1,2,24,1,3]{0,2,5,4,1,3:T(2,128)(2,1)} %copy.120), calls=%async_computation.5 | async-start | bytes 73728 | tf_op jit(solution)/shard_map/all_to_all | solution.py:114
where the time goes:
time: 131 us; the launch traced here: 130 us
  blocking collectives  59.5 us (45%)
  starting transfers between devices  26.3 us (20%)
  waiting for transfers between devices  22.5 us (17%)
  local copies, waits for them, and re-layouts  12.5 us (10%)
  other arithmetic  4.17 us (3%)
  matrix products  3.8 us (3%)
  between operations  1.69 us (1%)
    unnamed x4, blocking collectives  42.8 us
    all_to_all x2, waiting for transfers between devices, coarse_eval(): lax.all_to_all(coarse_grid_step(fourier), 'wave', split_axis=3, concat_ax...  11.7 us
    all_gather x2, blocking collectives, coarse_start(): gathered = lax.all_gather(modes, 'lev', axis=0, tiled=True)  10.4 us
    all_to_all x2, starting transfers between devices, coarse_eval(): lax.all_to_all(coarse_start(modes), 'wave', split_axis=5, concat_axis=3,...  9.25 us
    unnamed x26, local copies, waits for them, and re-layouts  7.27 us
    all_to_all x2, starting transfers between devices, coarse_eval(): lax.all_to_all(coarse_grid_step(fourier), 'wave', split_axis=3, concat_ax...  6.68 us
    all_to_all x1, starting transfers between devices, per_device(): lax.all_to_all(fine_fourier, 'wave', split_axis=5, concat_axis=3, tiled=T...  6.43 us
    all_gather x1, blocking collectives, per_device(): lax.all_gather(fine_state.astype(jnp.bfloat16), 'lev', axis=0, tiled=True)  6.21 us
  transfers between devices with their start and end apart: 6, of which 5 were waited for; matrix products, arithmetic and copies ran while one was open for 7% of the time, Pallas kernels for 0%

commit v1 on v0

--- a/solution.py
+++ b/solution.py
@@ -92,7 +92,8 @@
         return mix(modes_to, partial_sum)
 
     def coarse_start(modes):
-        gathered = lax.all_gather(modes, "lev", axis=0, tiled=True)
+        sent = jnp.stack([modes] * lax.axis_size("lev"))
+        gathered = jnp.concatenate(lax.all_to_all(sent, "lev", 0, 0), axis=0)
         levels = (mix(modes_from, gathered) * keep_float).astype(jnp.bfloat16)
         return legendre_inverse(levels, coarse_leg, keep_mask)
 

time: 131 us -> 137 us (1.046)
  blocking collectives: 59.5 us -> 49.3 us
  waiting for transfers between devices: 22.5 us -> 30.5 us
  starting transfers between devices: 26.3 us -> 30.1 us
  local copies, waits for them, and re-layouts: 12.5 us -> 15.3 us
    all_gather x2 -> x0, blocking collectives: 10.4 us -> none  [coarse_start(): gathered = lax.all_gather(modes, 'lev', axis=0, tiled=True)]
    all_to_all x0 -> x2, starting transfers between devices: none -> 6.45 us  [coarse_start(): gathered = jnp.concatenate(lax.all_to_all(sent, 'lev', 0, 0), axis=0)]
    all_to_all x2, waiting for transfers between devices: 5.53 us -> 10.3 us  [coarse_eval(): lax.all_to_all(coarse_start(modes), 'wave', split_axis=5, concat_axis=3,...]
    all_to_all x0 -> x2, waiting for transfers between devices: none -> 3.19 us  [coarse_start(): gathered = jnp.concatenate(lax.all_to_all(sent, 'lev', 0, 0), axis=0)]
    all_to_all x2, starting transfers between devices: 9.25 us -> 6.68 us  [coarse_eval(): lax.all_to_all(coarse_start(modes), 'wave', split_axis=5, concat_axis=3,...]
    unnamed x26 -> x32, local copies, waits for them, and re-layouts: 7.27 us -> 9.5 us
  transfers between devices with their start and end apart: 6 -> 8, of which waited for: 5 -> 8; matrix products, arithmetic and copies ran while one was open for 7% -> 10% of each run, Pallas kernels for 0% -> 0%
where the time goes in v1:
time: 137 us; the launch traced here: 136 us
  blocking collectives  49.3 us (36%)
  waiting for transfers between devices  30.5 us (22%)
  starting transfers between devices  30.1 us (22%)
  local copies, waits for them, and re-layouts  15.3 us (11%)
  other arithmetic  5.48 us (4%)
  matrix products  3.8 us (3%)
  between operations  1.77 us (1%)
    unnamed x4, blocking collectives  43.1 us
    all_to_all x2, waiting for transfers between devices, coarse_eval(): lax.all_to_all(coarse_grid_step(fourier), 'wave', split_axis=3, concat_ax...  11.7 us
    all_to_all x2, waiting for transfers between devices, coarse_eval(): lax.all_to_all(coarse_start(modes), 'wave', split_axis=5, concat_axis=3,...  10.3 us
    unnamed x32, local copies, waits for them, and re-layouts  9.5 us
    all_to_all x2, starting transfers between devices, coarse_eval(): lax.all_to_all(coarse_start(modes), 'wave', split_axis=5, concat_axis=3,...  6.68 us
    all_to_all x2, starting transfers between devices, coarse_eval(): lax.all_to_all(coarse_grid_step(fourier), 'wave', split_axis=3, concat_ax...  6.68 us
    all_to_all x2, starting transfers between devices, coarse_start(): gathered = jnp.concatenate(lax.all_to_all(sent, 'lev', 0, 0), axis=0)  6.45 us
    all_to_all x1, starting transfers between devices, per_device(): lax.all_to_all(fine_fourier, 'wave', split_axis=5, concat_axis=3, tiled=T...  6.43 us
  transfers between devices with their start and end apart: 8, of which 8 were waited for; matrix products, arithmetic and copies ran while one was open for 10% of the time, Pallas kernels for 0%

profile of v1, /device:TPU:0, one launch (start us, length us, event | category | flops | bytes accessed | tf_op | source)
XLA Modules:
  0.0 136.3 jit_solution(5797076958305102702)
XLA Ops:
  0.7 0.7 broadcast_subtract_fusion.1
  1.5 6.2 %all_gather.3 = bf16[8,3,2,3,49]{4,2,3,1,0:T(2,128)(2,1)S(1)} all-gather(bf16[2,3,2,3,49]{4,2,3,1,0:T(2,128)(2,1)S(1)} %convert_element_type.212), channel_id=1, replica_groups=mesh['wave'=8,'lev'=4] {'lev'}, dimensions={0}, use_global_device_ids=true | all-gather | bytes 17640 | tf_op jit(solution)/shard_map/all_gather | solution.py:121
  7.7 0.7 copy-done.1
  8.4 0.1 fusion.2
  8.6 0.2 copy.99
  8.7 0.8 reshape.482
  9.6 6.4 %all-to-all-start = ((bf16[8,2,432]{2,1,0:T(2,128)(2,1)}), bf16[8,2,432]{2,1,0:T(2,128)(2,1)S(1)}, u32[]{:S(2)}, u32[]{:S(2)}) async-start(bf16[8,2,432]{2,1,0:T(2,128)(2,1)} %reshape.482), calls=%async_computation | async-start | bytes 32768 | tf_op jit(solution)/shard_map/all_to_all | solution.py:123
  16.1 0.6 multiply_convert_fusion.3
  16.7 2.3 %multiply_convert_fusion.1 = (bf16[1,24,2,2560]{3,1,2,0:T(8,128)(2,1)S(1)}, bf16[1,24,2,2560]{3,1,2,0:T(8,128)(2,1)S(1)}) fusion(s32[24,2]{0,1:T(2,128)S(1)} %pad_add_fusion), kind=kLoop, calls=%fused_computation.52 | loop fusion | flops 1720320 | bytes 491712 | tf_op jit(solution)/shard_map/convert.4
  19.1 0.6 copy-done.6
  19.9 0.6 copy-done.7
  20.5 2.1 %all-to-all-done = bf16[8,2,432]{2,1,0:T(2,128)(2,1)S(1)} async-done(((bf16[8,2,432]{2,1,0:T(2,128)(2,1)}), bf16[8,2,432]{2,1,0:T(2,128)(2,1)S(1)}, u32[]{:S(2)}, u32[]{:S(2)}) %all-to-all-start) | async-done | bytes 13856 | tf_op jit(solution)/shard_map/all_to_all | solution.py:123
  22.6 0.2 reshape.483
  22.8 0.2 copy.101
  23.0 0.7 copy-done.3
  23.7 0.8 fusion.3
  24.6 0.2 copy.103
  24.7 0.8 reshape.484
  25.6 3.9 %all-to-all-start.1 = ((bf16[8,2,432]{2,1,0:T(2,128)(2,1)}), bf16[8,2,432]{2,1,0:T(2,128)(2,1)S(1)}, u32[]{:S(2)}, u32[]{:S(2)}) async-start(bf16[8,2,432]{2,1,0:T(2,128)(2,1)} %reshape.484), calls=%async_computation.1 | async-start | bytes 32768 | tf_op jit(solution)/shard_map/all_to_all | solution.py:124
  29.5 1.4 %slice.60 = f32[8,1280]{1,0:T(8,128)S(1)} slice(f32[8,2560]{1,0:T(8,128)S(1)} %copy-done.3), slice={[0:8:1], [0:2560:2]} | slice | bytes 81920 | tf_op jit(solution)/shard_map/slice | solution.py:85
  31.0 0.6 copy-done.8
  31.6 0.6 dynamic-slice
  32.9 3.2 %all-to-all-done.1 = bf16[8,2,432]{2,1,0:T(2,128)(2,1)S(1)} async-done(((bf16[8,2,432]{2,1,0:T(2,128)(2,1)}), bf16[8,2,432]{2,1,0:T(2,128)(2,1)S(1)}, u32[]{:S(2)}, u32[]{:S(2)}) %all-to-all-start.1) | async-done | bytes 13856 | tf_op jit(solution)/shard_map/all_to_all | solution.py:124
  36.0 0.2 reshape.485
  36.3 0.2 copy.105
  36.4 0.2 fusion
  36.7 10.5 %all-reduce.1 = bf16[8,3,2,3,49]{4,0,3,2,1:T(8,128)(2,1)S(1)} all-reduce(bf16[8,3,2,3,49]{4,0,3,2,1:T(8,128)(2,1)S(1)} %copy.107), channel_id=2, replica_groups=mesh['wave'=8,'lev'=4] {'lev'}, use_global_device_ids=true, to_apply=%region_1.2.clone | all-reduce | flops 7056 | bytes 28224
  47.2 0.3 convolution_convert_fusion
  47.6 11.7 %all-reduce.2 = bf16[8,6,2,3,24]{4,0,3,2,1:T(8,128)(2,1)S(1)} all-reduce(bf16[8,6,2,3,24]{4,0,3,2,1:T(8,128)(2,1)S(1)} %convolution_convert_fusion), channel_id=3, replica_groups=mesh['wave'=8,'lev'=4] {'lev'}, use_global_device_ids=true, to_apply=%region_2.3.clone | all-reduce | flops 6912 | bytes 27648
  59.4 0.7 reshape.488
  60.1 3.2 %all-to-all-start.2 = ((f32[4,1,288]{2,1,0:T(1,128)}), f32[4,1,288]{2,1,0:T(1,128)S(1)}, u32[]{:S(2)}, u32[]{:S(2)}) async-start(f32[4,1,288]{2,1,0:T(1,128)} %reshape.488), calls=%async_computation.2 | async-start | bytes 12288 | tf_op jit(solution)/shard_map/all_to_all | solution.py:96
  63.3 0.6 copy.129
  63.9 0.7 reshape.486
  64.6 2.4 %all-to-all-done.2 = f32[4,1,288]{2,1,0:T(1,128)S(1)} async-done(((f32[4,1,288]{2,1,0:T(1,128)}), f32[4,1,288]{2,1,0:T(1,128)S(1)}, u32[]{:S(2)}, u32[]{:S(2)}) %all-to-all-start.2) | async-done | bytes 4640 | tf_op jit(solution)/shard_map/all_to_all | solution.py:96
  67.1 3.2 %all-to-all-start.5 = ((f32[4,1,288]{2,1,0:T(1,128)}), f32[4,1,288]{2,1,0:T(1,128)S(1)}, u32[]{:S(2)}, u32[]{:S(2)}) async-start(f32[4,1,288]{2,1,0:T(1,128)} %reshape.486), calls=%async_computation.5 | async-start | bytes 12288 | tf_op jit(solution)/shard_map/all_to_all | solution.py:96
  70.3 0.5 broadcast.461
  70.9 0.7 reduce.2
  71.7 0.7 copy-done.4
  72.3 0.2 fusion.23
  72.6 0.7 copy.110
  73.3 0.8 all-to-all-done.5
  74.1 3.3 %all-to-all-start.3 = ((bf16[8,1,2,3,1,24]{0,2,3,4,1,5:T(2,128)(2,1)}), bf16[8,1,2,3,1,24]{0,2,3,4,1,5:T(2,128)(2,1)S(1)}, u32[]{:S(2)}, u32[]{:S(2)}) async-start(bf16[8,1,2,3,1,24]{0,2,3,4,1,5:T(2,128)(2,1)} %copy.110), calls=%async_computation.3 | async-start | bytes 73728 | tf_op jit(solution)/shard_map/all_to_all | solution.py:112
  77.4 0.7 reduce.1
  78.2 0.2 fusion.20
  78.5 0.7 copy.120
  79.2 4.9 %all-to-all-done.3 = bf16[8,1,2,3,1,24]{0,2,3,4,1,5:T(2,128)(2,1)S(1)} async-done(((bf16[8,1,2,3,1,24]{0,2,3,4,1,5:T(2,128)(2,1)}), bf16[8,1,2,3,1,24]{0,2,3,4,1,5:T(2,128)(2,1)S(1)}, u32[]{:S(2)}, u32[]{:S(2)}) %all-to-all-start.3) | async-done | bytes 2336 | tf_op jit(solution)/shard_map/all_to_all | solution.py:112
  84.1 3.3 %all-to-all-start.6 = ((bf16[8,1,2,3,1,24]{0,2,3,4,1,5:T(2,128)(2,1)}), bf16[8,1,2,3,1,24]{0,2,3,4,1,5:T(2,128)(2,1)S(1)}, u32[]{:S(2)}, u32[]{:S(2)}) async-start(bf16[8,1,2,3,1,24]{0,2,3,4,1,5:T(2,128)(2,1)} %copy.120), calls=%async_computation.6 | async-start | bytes 73728 | tf_op jit(solution)/shard_map/all_to_all | solution.py:112
  87.5 0.4 fusion.21
  87.9 0.8 copy.114
  88.6 5.5 %all-to-all-done.6 = bf16[8,1,2,3,1,24]{0,2,3,4,1,5:T(2,128)(2,1)S(1)} async-done(((bf16[8,1,2,3,1,24]{0,2,3,4,1,5:T(2,128)(2,1)}), bf16[8,1,2,3,1,24]{0,2,3,4,1,5:T(2,128)(2,1)S(1)}, u32[]{:S(2)}, u32[]{:S(2)}) %all-to-all-start.6) | async-done | bytes 2336 | tf_op jit(solution)/shard_map/all_to_all | solution.py:112
  94.1 3.3 %all-to-all-start.4 = ((bf16[8,1,2,24,1,3]{0,2,5,4,1,3:T(2,128)(2,1)}), bf16[8,1,2,24,1,3]{0,2,5,4,1,3:T(2,128)(2,1)S(1)}, u32[]{:S(2)}, u32[]{:S(2)}) async-start(bf16[8,1,2,24,1,3]{0,2,5,4,1,3:T(2,128)(2,1)} %copy.114), calls=%async_computation.4 | async-start | bytes 73728 | tf_op jit(solution)/shard_map/all_to_all | solution.py:115
  97.5 0.4 fusion.18
  97.9 0.8 copy.124
  98.6 5.5 %all-to-all-done.4 = bf16[8,1,2,24,1,3]{0,2,5,4,1,3:T(2,128)(2,1)S(1)} async-done(((bf16[8,1,2,24,1,3]{0,2,5,4,1,3:T(2,128)(2,1)}), bf16[8,1,2,24,1,3]{0,2,5,4,1,3:T(2,128)(2,1)S(1)}, u32[]{:S(2)}, u32[]{:S(2)}) %all-to-all-start.4) | async-done | bytes 2336 | tf_op jit(solution)/shard_map/all_to_all | solution.py:115
  104.1 3.3 %all-to-all-start.7 = ((bf16[8,1,2,24,1,3]{0,2,5,4,1,3:T(2,128)(2,1)}), bf16[8,1,2,24,1,3]{0,2,5,4,1,3:T(2,128)(2,1)S(1)}, u32[]{:S(2)}, u32[]{:S(2)}) async-start(bf16[8,1,2,24,1,3]{0,2,5,4,1,3:T(2,128)(2,1)} %copy.124), calls=%async_computation.7 | async-start | bytes 73728 | tf_op jit(solution)/shard_map/all_to_all | solution.py:115
  107.5 0.2 fusion.7
  107.7 0.2 fusion.15
  107.8 6.2 %all-to-all-done.7 = bf16[8,1,2,24,1,3]{0,2,5,4,1,3:T(2,128)(2,1)S(1)} async-done(((bf16[8,1,2,24,1,3]{0,2,5,4,1,3:T(2,128)(2,1)}), bf16[8,1,2,24,1,3]{0,2,5,4,1,3:T(2,128)(2,1)S(1)}, u32[]{:S(2)}, u32[]{:S(2)}) %all-to-all-start.7) | async-done | bytes 2336 | tf_op jit(solution)/shard_map/all_to_all | solution.py:115
  114.1 0.2 fusion.9
  114.3 0.2 fusion.17
  114.5 10.3 %all-reduce.6 = (bf16[8,1,2,3,24]{4,0,3,2,1:T(8,128)(2,1)S(1)}, bf16[8,1,2,3,24]{4,0,3,2,1:T(8,128)(2,1)S(1)}) all-reduce(bf16[8,1,2,3,24]{4,0,3,2,1:T(8,128)(2,1)S(1)} %fusion.17, bf16[8,1,2,3,24]{4,0,3,2,1:T(8,128)(2,1)S(1)} %fusion.15), channel_id=5, replica_groups=mesh['wave'=8,'lev'=4] {'lev'}, use_global_device_ids=true, to_apply=%region_4.5.clone | all-reduce | flops 2304 | bytes 9216
  124.8 0.2 convolution_convert_fusion.2
  125.0 10.6 %all-reduce.5 = bf16[8,2,2,3,24]{4,0,3,2,1:T(8,128)(2,1)S(1)} all-reduce(bf16[8,2,2,3,24]{4,0,3,2,1:T(8,128)(2,1)S(1)} %convolution_convert_fusion.2), channel_id=6, replica_groups=mesh['wave'=8,'lev'=4] {'lev'}, use_global_device_ids=true, to_apply=%region_5.6.clone | all-reduce | flops 2304 | bytes 9216
  135.7 0.6 copy.128
  (50 shorter events, 1.3 us)
Async XLA Ops:
  0.6 46.6 %copy-start = (f32[8,8]{1,0:T(8,128)S(1)}, f32[8,8]{1,0:T(8,128)}, u32[]{:S(2)}) copy-start(f32[8,8]{1,0:T(8,128)} %param.14) | copy-start | bytes 772
  0.6 0.8 copy-start.2
  7.7 0.7 copy-start.1
  9.6 6.4 %copy-start.5 = (s32[24]{0:T(128)S(1)}, s32[24]{0:T(128)}, u32[]{:S(2)}) copy-start(s32[24]{0:T(128)} %param.9) | copy-start | bytes 292
  9.6 13.0 %all-to-all-start = ((bf16[8,2,432]{2,1,0:T(2,128)(2,1)}), bf16[8,2,432]{2,1,0:T(2,128)(2,1)S(1)}, u32[]{:S(2)}, u32[]{:S(2)}) async-start(bf16[8,2,432]{2,1,0:T(2,128)(2,1)} %reshape.482), calls=%async_computation | async-start | bytes 32768 | tf_op jit(solution)/shard_map/all_to_all | solution.py:123
  19.0 0.7 copy-start.6
  19.8 0.7 copy-start.7
  22.8 0.9 copy-start.3
  25.6 10.5 %all-to-all-start.1 = ((bf16[8,2,432]{2,1,0:T(2,128)(2,1)}), bf16[8,2,432]{2,1,0:T(2,128)(2,1)S(1)}, u32[]{:S(2)}, u32[]{:S(2)}) async-start(bf16[8,2,432]{2,1,0:T(2,128)(2,1)} %reshape.484), calls=%async_computation.1 | async-start | bytes 32768 | tf_op jit(solution)/shard_map/all_to_all | solution.py:124
  31.0 0.7 copy-start.8
  60.1 7.0 %all-to-all-start.2 = ((f32[4,1,288]{2,1,0:T(1,128)}), f32[4,1,288]{2,1,0:T(1,128)S(1)}, u32[]{:S(2)}, u32[]{:S(2)}) async-start(f32[4,1,288]{2,1,0:T(1,128)} %reshape.488), calls=%async_computation.2 | async-start | bytes 12288 | tf_op jit(solution)/shard_map/all_to_all | solution.py:96
  67.1 7.0 %all-to-all-start.5 = ((f32[4,1,288]{2,1,0:T(1,128)}), f32[4,1,288]{2,1,0:T(1,128)S(1)}, u32[]{:S(2)}, u32[]{:S(2)}) async-start(f32[4,1,288]{2,1,0:T(1,128)} %reshape.486), calls=%async_computation.5 | async-start | bytes 12288 | tf_op jit(solution)/shard_map/all_to_all | solution.py:96
  71.6 0.7 copy-start.4
  74.1 10.0 %all-to-all-start.3 = ((bf16[8,1,2,3,1,24]{0,2,3,4,1,5:T(2,128)(2,1)}), bf16[8,1,2,3,1,24]{0,2,3,4,1,5:T(2,128)(2,1)S(1)}, u32[]{:S(2)}, u32[]{:S(2)}) async-start(bf16[8,1,2,3,1,24]{0,2,3,4,1,5:T(2,128)(2,1)} %copy.110), calls=%async_computation.3 | async-start | bytes 73728 | tf_op jit(solution)/shard_map/all_to_all | solution.py:112
  84.1 10.0 %all-to-all-start.6 = ((bf16[8,1,2,3,1,24]{0,2,3,4,1,5:T(2,128)(2,1)}), bf16[8,1,2,3,1,24]{0,2,3,4,1,5:T(2,128)(2,1)S(1)}, u32[]{:S(2)}, u32[]{:S(2)}) async-start(bf16[8,1,2,3,1,24]{0,2,3,4,1,5:T(2,128)(2,1)} %copy.120), calls=%async_computation.6 | async-start | bytes 73728 | tf_op jit(solution)/shard_map/all_to_all | solution.py:112
  94.1 10.0 %all-to-all-start.4 = ((bf16[8,1,2,24,1,3]{0,2,5,4,1,3:T(2,128)(2,1)}), bf16[8,1,2,24,1,3]{0,2,5,4,1,3:T(2,128)(2,1)S(1)}, u32[]{:S(2)}, u32[]{:S(2)}) async-start(bf16[8,1,2,24,1,3]{0,2,5,4,1,3:T(2,128)(2,1)} %copy.114), calls=%async_computation.4 | async-start | bytes 73728 | tf_op jit(solution)/shard_map/all_to_all | solution.py:115
  104.1 10.0 %all-to-all-start.7 = ((bf16[8,1,2,24,1,3]{0,2,5,4,1,3:T(2,128)(2,1)}), bf16[8,1,2,24,1,3]{0,2,5,4,1,3:T(2,128)(2,1)S(1)}, u32[]{:S(2)}, u32[]{:S(2)}) async-start(bf16[8,1,2,24,1,3]{0,2,5,4,1,3:T(2,128)(2,1)} %copy.124), calls=%async_computation.7 | async-start | bytes 73728 | tf_op jit(solution)/shard_map/all_to_all | solution.py:115
